TPU v7x, 256 devices: a whole 4x4x8 slice. The times are simulated.
256 devices in a mesh: blk: 32 (over x_lo, z, core), tp: 8 (over x_hi, y).
Axes of the slice: x: 4 (x_hi: 2, x_lo: 2; x = x_hi * 2 + x_lo), y: 4, z: 8, core: 2. Of those that a mesh axis runs over, the one named last changes fastest.
Arguments:
- tokens: bfloat16 [8192, 8192], P('blk', 'tp'), may hold values from -6 to 6
- weight: bfloat16 [8192, 2048], P('tp'), may hold values from -0.0625 to 0.0625
- bank_a: bfloat16 [32, 8192, 32], P('blk', 'tp'), may hold values from -0.0625 to 0.0625
- bank_b: bfloat16 [32, 32, 1024], P('blk'), may hold values from -1.5 to 1.5
- tile_map: int32 [64, 1], P('blk'), may hold values from 0 to 31
- grad_out: bfloat16 [8192, 2048], P(('blk', 'tp')), may hold values from -6 to 6
Outputs:
- key_value_output: bfloat16 [8192, 2048], P(('blk', 'tp'))
- token_gradient: bfloat16 [8192, 8192], P('blk', 'tp')
- grad_a: float32 [32, 8192, 32], P('blk', 'tp')
- grad_b: float32 [32, 32, 1024], P('blk', None, 'tp')
Inputs may be any that keep to these rules, and one draw needn't show every extreme that they name: `tile_map`: every one of the 32 adapters is the adapter of at least one tile.
All inputs are finite; a program needn't handle non-finite values.
Results may differ from a plain program's by a relative error of at most 0.003.
Values may be sent and summed in bfloat16 or wider, within the bound.
A program may use at most 64 MiB of HBM per device.

v0:
```python
import jax
import jax.numpy as jnp
from jax import lax
from jax.sharding import PartitionSpec as P

adapter_scale = 0.5


def on_device(tokens, weight, bank_a, bank_b, tile_map, grad_out):
    tile_index_list = tile_map[:, 0]
    grouped_row_count = tokens.shape[0]
    feature_shard = tokens.shape[1]
    tile_count = tile_index_list.shape[0]
    tile_rows = grouped_row_count // tile_count
    rank_two = bank_a.shape[2]
    rank_one = rank_two // 2
    kv_width = bank_b.shape[2]
    tp_count = lax.axis_size("tp")
    local_row_block = grouped_row_count // tp_count
    kv_dev = kv_width // tp_count
    adapt_local = bank_a.shape[0]
    empty = (
        jnp.zeros((tile_count, feature_shard, rank_two), jnp.bfloat16),
        jnp.zeros((tile_count, rank_two, kv_width), jnp.bfloat16),
    )
    whole_a, whole_b = (
        lax.all_gather(bank_a, "blk", axis=0, tiled=True),
        lax.all_gather(bank_b, "blk", axis=0, tiled=True),
    )
    pieces = (whole_a, whole_b)
    piece_rows = pieces[0].shape[0]
    one_hot = (tile_index_list[:, None] == jnp.arange(piece_rows, dtype=jnp.int32)[None, :]).astype(
        jnp.bfloat16
    )
    picked_a = jnp.dot(
        one_hot, pieces[0].reshape(piece_rows, -1), preferred_element_type=jnp.float32
    )
    picked_b = jnp.dot(
        one_hot, pieces[1].reshape(piece_rows, -1), preferred_element_type=jnp.float32
    )
    factor_down = picked_a.reshape(empty[0].shape).astype(jnp.bfloat16)
    fac_b = picked_b.reshape(empty[1].shape).astype(jnp.bfloat16)
    token_tile_index = tokens.reshape(tile_count, tile_rows, feature_shard)
    rank_part = jnp.einsum(
        "tre,tek->trk", token_tile_index, factor_down, preferred_element_type=jnp.float32
    )
    rank_act = lax.psum(rank_part, "tp").astype(jnp.bfloat16)
    base_local_rows = lax.psum_scatter(
        jnp.dot(tokens, weight, preferred_element_type=jnp.float32),
        "tp",
        scatter_dimension=0,
        tiled=True,
    )
    adapter_complete = jnp.concatenate(
        [
            jnp.einsum(
                "trk,tkc->trc",
                rank_act[:, :, :rank_one],
                fac_b[:, :rank_one],
                preferred_element_type=jnp.float32,
            ),
            jnp.einsum(
                "trk,tkc->trc",
                rank_act[:, :, rank_one:],
                fac_b[:, rank_one:],
                preferred_element_type=jnp.float32,
            ),
        ],
        axis=2,
    ).reshape(grouped_row_count, 2 * kv_width)
    first_row_index = lax.axis_index("tp") * local_row_block
    adapter_local_rows = lax.dynamic_slice_in_dim(
        adapter_complete, first_row_index, local_row_block, 0
    )
    key_value_output = (base_local_rows + adapter_scale * adapter_local_rows).astype(jnp.bfloat16)
    grad_rows = lax.all_gather(grad_out, "tp", axis=0, tiled=True)
    gradient_per_tile = grad_rows.reshape(tile_count, tile_rows, 2 * kv_width)
    low_rank_gradient = jnp.concatenate(
        [
            jnp.einsum(
                "trc,tkc->trk",
                gradient_per_tile[:, :, :kv_width],
                fac_b[:, :rank_one],
                preferred_element_type=jnp.float32,
            ),
            jnp.einsum(
                "trc,tkc->trk",
                gradient_per_tile[:, :, kv_width:],
                fac_b[:, rank_one:],
                preferred_element_type=jnp.float32,
            ),
        ],
        axis=2,
    ).astype(jnp.bfloat16)
    backward_pass = jnp.einsum("rc,ec->re", grad_rows, weight, preferred_element_type=jnp.float32)
    backward_adapter_term = jnp.einsum(
        "qdu,qyu->qdy", low_rank_gradient, factor_down, preferred_element_type=jnp.float32
    )
    token_gradient = (
        backward_pass
        + adapter_scale * backward_adapter_term.reshape(grouped_row_count, feature_shard)
    ).astype(jnp.bfloat16)
    tile_down_gradient = adapter_scale * jnp.einsum(
        "tre,trk->tek", token_tile_index, low_rank_gradient, preferred_element_type=jnp.float32
    )
    col_start = lax.axis_index("tp") * kv_dev
    key_cols = lax.dynamic_slice_in_dim(gradient_per_tile[:, :, :kv_width], col_start, kv_dev, 2)
    value_cols = lax.dynamic_slice_in_dim(gradient_per_tile[:, :, kv_width:], col_start, kv_dev, 2)
    tile_up_gradient = adapter_scale * jnp.concatenate(
        [
            jnp.einsum(
                "trk,trc->tkc",
                rank_act[:, :, :rank_one],
                key_cols,
                preferred_element_type=jnp.float32,
            ),
            jnp.einsum(
                "trk,trc->tkc",
                rank_act[:, :, rank_one:],
                value_cols,
                preferred_element_type=jnp.float32,
            ),
        ],
        axis=1,
    )
    size_a = feature_shard * rank_two
    flat_grads = jnp.concatenate(
        [tile_down_gradient.reshape(tile_count, -1), tile_up_gradient.reshape(tile_count, -1)],
        axis=1,
    )
    one_hot = (
        tile_index_list[:, None]
        == jnp.arange(adapt_local * lax.axis_size("blk"), dtype=jnp.int32)[None, :]
    ).astype(jnp.float32)
    summed = lax.psum_scatter(
        jnp.dot(
            one_hot.T,
            flat_grads,
            precision=lax.Precision.HIGHEST,
            preferred_element_type=jnp.float32,
        ),
        "blk",
        scatter_dimension=0,
        tiled=True,
    )
    grad_a = summed[:, :size_a].reshape(adapt_local, feature_shard, rank_two)
    grad_b = summed[:, size_a:].reshape(adapt_local, rank_two, kv_dev)
    return (key_value_output, token_gradient, grad_a, grad_b)


def solution(mesh):
    in_specs = (
        P("blk", "tp"),
        P("tp", None),
        P("blk", "tp", None),
        P("blk", None, None),
        P("blk", None),
        P(("blk", "tp"), None),
    )
    out_specs = (P(("blk", "tp"), None), P("blk", "tp"), P("blk", "tp", None), P("blk", None, "tp"))
    return jax.shard_map(
        on_device, mesh=mesh, in_specs=in_specs, out_specs=out_specs, check_vma=False
    )
```

profile of v0, /device:TPU:1, one launch (start us, length us, event | category | flops | bytes accessed | tf_op | source)
XLA Modules:
  0.0 530.9 jit_solution(16734941255564982452)
XLA Ops:
  7.2 0.7 all-gather.8.cloned.1.call-update
  8.0 0.7 all-gather.4.cloned.1.call-update
  8.7 0.7 all-gather.6.cloned.1.call-update
  9.5 4.8 fusion.45
  14.3 50.2 %all-gather.8.cloned.1.call-done = bf16[256,2048]{1,0:T(8,128)(2,1)} async-done(((bf16[32,2048]{1,0:T(8,128)(2,1)}), bf16[256,2048]{1,0:T(8,128)(2,1)}) %all-gather.8.cloned.1.call-update) | async-done | bytes 1048592 | tf_op jit(solution)/shard_map/all_gather | solution.py:76
  64.5 2.1 fusion.43
  66.6 65.2 %all-gather.4.cloned.1.call-done = bf16[32,1024,32]{1,2,0:T(8,128)(2,1)} async-done(((bf16[1,1024,32]{1,2,0:T(8,128)(2,1)}), bf16[32,1024,32]{1,2,0:T(8,128)(2,1)}) %all-gather.4.cloned.1.call-update) | async-done | bytes 2097168 | tf_op jit(solution)/shard_map/all_gather | solution.py:27
  131.7 7.8 %copy.28 = bf16[32,1024,32]{2,1,0:T(8,128)(2,1)} copy(bf16[32,1024,32]{1,2,0:T(8,128)(2,1)} %all-gather.4.cloned.1.call-done) | data formatting | bytes 4194304 | tf_op jit(solution)/shard_map/all_gather | solution.py:27
  139.5 10.5 %reshape.43 = bf16[32,32768]{1,0:T(8,128)(2,1)S(1)} reshape(bf16[32,1024,32]{2,1,0:T(8,128)(2,1)} %copy.28) | data formatting | bytes 4194304 | tf_op jit(solution)/shard_map/reshape | solution.py:36
  150.0 8.0 %dot_general.58 = bf16[1024,32,32]{1,0,2:T(8,128)(2,1)} reshape(bf16[32768,32]{0,1:T(8,128)(2,1)S(1)} %bitcast.50) | data formatting | bytes 4194304 | tf_op jit(solution)/shard_map/dot_general | solution.py:35
  158.1 7.5 %copy.29 = bf16[1024,32,32]{0,2,1:T(8,128)(2,1)S(1)} copy(bf16[1024,32,32]{1,0,2:T(8,128)(2,1)} %dot_general.58) | data formatting | bytes 4194304 | tf_op jit(solution)/shard_map/dot_general | solution.py:35
  166.3 34.4 %psum.7 = bf16[2,128,32]{1,2,0:T(8,128)(2,1)S(1)} all-reduce(f32[2,128,32]{1,2,0:T(8,128)S(1)} %convolution_bitcast_fusion), channel_id=1, replica_groups=mesh['blk'=32,'tp'=8] {'tp'}, use_global_device_ids=true, to_apply=%region_1.0 | all-reduce | flops 8192 | bytes 49152 | tf_op jit(solution)/shard_map/psum | solution.py:47
  200.7 1.0 fusion.16
  201.9 3.9 fusion.5
  207.5 3.9 fusion.10
  211.4 0.6 copy-done.5
  213.9 1.7 copy-done.4
  215.9 2.1 fusion.3
  218.0 61.8 %reduce-scatter.2.cloned.1.call-done = f32[32,2048]{1,0:T(8,128)} async-done(((f32[256,2048]{1,0:T(8,128)}), f32[32,2048]{1,0:T(8,128)}) %reduce-scatter.2.cloned.1.call-update) | async-done | bytes 262160 | tf_op jit(solution)/shard_map/reduce_scatter | solution.py:48
  279.8 1.6 add_convert_fusion
  281.4 237.6 %all-reduce.3.cloned.1.call-done = f32[32,36864]{1,0:T(8,128)} async-done(((f32[32,36864]{1,0:T(8,128)}), f32[32,36864]{1,0:T(8,128)}) %all-reduce.3.cloned.1.call-update) | async-done | bytes 4718608
  519.0 2.1 dynamic-slice_reduce_fusion
  521.3 0.8 copy.38
  522.2 2.2 dynamic-slice.3
  (35 shorter events, 5.2 us)
Async XLA Ops:
  7.2 2.3 copy-start
  7.2 57.3 %all-gather.8.cloned.1.call-start = ((), (), s32[]{:S(2)}) async-start(), calls=%async_computation.4 | async-start | bytes 1179648 | tf_op jit(solution)/shard_map/all_gather | solution.py:76
  7.9 123.8 %all-gather.4.cloned.1.call-start = ((), (), s32[]{:S(2)}) async-start(), calls=%async_computation.2 | async-start | bytes 2162688 | tf_op jit(solution)/shard_map/all_gather | solution.py:27
  8.7 193.2 %all-gather.6.cloned.1.call-start = ((), (), s32[]{:S(2)}) async-start(), calls=%async_computation.3 | async-start | bytes 2162688 | tf_op jit(solution)/shard_map/all_gather | solution.py:28
  9.4 270.4 %reduce-scatter.2.cloned.1.call-start = ((), (), s32[]{:S(2)}) async-start(), calls=%async_computation.1 | async-start | bytes 2359296 | tf_op jit(solution)/shard_map/reduce_scatter | solution.py:48
  14.2 504.8 %all-reduce.3.cloned.1.call-start = ((), (), s32[]{:S(2)}) async-start(), calls=%async_computation.5 | async-start | bytes 9437184
  158.1 7.5 %copy-start.3 = (s32[2,1]{0,1:T(1,128)S(1)}, s32[2,1]{0,1:T(1,128)}, u32[]{:S(2)}) copy-start(s32[2,1]{0,1:T(1,128)} %param.10) | copy-start | bytes 28
  166.1 39.8 %copy-start.1 = (bf16[256,2048]{1,0:T(8,128)(2,1)S(1)}, bf16[256,2048]{1,0:T(8,128)(2,1)}, u32[]{:S(2)}) copy-start(bf16[256,2048]{1,0:T(8,128)(2,1)} %all-gather.8.cloned.1.call-done) | copy-start | bytes 3145732
  211.4 0.7 copy-start.5
  213.4 2.2 copy-start.4
  213.7 2.2 copy-start.2
Sparse Core Ops, SparseCore 0:
  10.7 53.7 all-gather.7
  66.3 65.3 all-gather.3
  133.6 64.5 all-gather.5
  202.0 77.7 reduce-scatter.1
  282.3 236.6 all-reduce.2
where the time goes:
time: 532 us; the launch traced here: 531 us
  waiting for transfers between devices  417 us (78%)
  local copies, waits for them, and re-layouts  45.6 us (9%)
  blocking collectives  34.4 us (6%)
  matrix products  18.2 us (3%)
  between operations  13.9 us (3%)
    unnamed x6, waiting for transfers between devices  240 us
    all_gather x1, waiting for transfers between devices, on_device(): lax.all_gather(bank_a, 'blk', axis=0, tiled=True)  65.2 us
    reduce_scatter x1, waiting for transfers between devices, on_device(): lax.psum_scatter(jnp.dot(tokens, weight, preferred_element_type=jnp.float...  61.8 us
    all_gather x1, waiting for transfers between devices, on_device(): grad_rows = lax.all_gather(grad_out, 'tp', axis=0, tiled=True)  50.2 us
    psum x1, blocking collectives, on_device(): rank_act = lax.psum(rank_part, 'tp').astype(jnp.bfloat16)  34.4 us
    dot_general x2, local copies, waits for them, and re-layouts, on_device(): jnp.dot(one_hot, pieces[0].reshape(piece_rows, -1), preferred_element_typ...  15.6 us
  transfers between devices with their start and end apart: 5, of which 4 were waited for; matrix products, arithmetic and copies ran while one was open for 11% of the time, Pallas kernels for 0%

commit v1 on v0

--- a/solution.py
+++ b/solution.py
@@ -24,7 +24,9 @@
         jnp.zeros((tile_count, rank_two, kv_width), jnp.bfloat16),
     )
     whole_a, whole_b = (
-        lax.all_gather(bank_a, "blk", axis=0, tiled=True),
+        jnp.concatenate(
+            lax.all_to_all(jnp.stack([bank_a] * lax.axis_size("blk")), "blk", 0, 0), axis=0
+        ),
         lax.all_gather(bank_b, "blk", axis=0, tiled=True),
     )
     pieces = (whole_a, whole_b)

time: 532 us -> 470 us (0.88)
  waiting for transfers between devices: 417 us -> 345 us
  starting transfers between devices: 0.19 us -> 11.2 us
    all_gather x1 -> x0, waiting for transfers between devices: 65.2 us -> none  [on_device(): lax.all_gather(bank_a, 'blk', axis=0, tiled=True)]
    another operation x0 -> x2, local copies, waits for them, and re-layouts: none -> 13 us  [the longest x1 10.5 us: on_device(): pieces[0].reshape(piece_rows, -1)]
    all_to_all x0 -> x1, starting transfers between devices: none -> 11.1 us  [on_device(): lax.all_to_all(jnp.stack([bank_a] * lax.axis_size('blk')), 'blk', 0, 0)]
    reshape x1 -> x0, local copies, waits for them, and re-layouts: 10.5 us -> none  [on_device(): pieces[0].reshape(piece_rows, -1)]
    all_gather x1 -> x0, local copies, waits for them, and re-layouts: 7.76 us -> none  [on_device(): lax.all_gather(bank_a, 'blk', axis=0, tiled=True)]
    all_to_all x0 -> x1, local copies, waits for them, and re-layouts: none -> 5.97 us  [on_device(): lax.all_to_all(jnp.stack([bank_a] * lax.axis_size('blk')), 'blk', 0, 0)]
    all_gather x1, waiting for transfers between devices: 50.2 us -> 44.2 us  [on_device(): grad_rows = lax.all_gather(grad_out, 'tp', axis=0, tiled=True)]
    unnamed x6 -> x5, waiting for transfers between devices: 240 us -> 239 us
  transfers between devices with their start and end apart: 5 -> 5, of which waited for: 4 -> 3; matrix products, arithmetic and copies ran while one was open for 11% -> 12% of each run, Pallas kernels for 0% -> 0%
where the time goes in v1:
time: 470 us; the launch traced here: 469 us
  waiting for transfers between devices  345 us (73%)
  local copies, waits for them, and re-layouts  46.4 us (10%)
  blocking collectives  32.9 us (7%)
  matrix products  18.2 us (4%)
  between operations  13.9 us (3%)
  starting transfers between devices  11.2 us (2%)
    unnamed x5, waiting for transfers between devices  239 us
    reduce_scatter x1, waiting for transfers between devices, on_device(): lax.psum_scatter(jnp.dot(tokens, weight, preferred_element_type=jnp.float...  61.5 us
    all_gather x1, waiting for transfers between devices, on_device(): grad_rows = lax.all_gather(grad_out, 'tp', axis=0, tiled=True)  44.2 us
    psum x1, blocking collectives, on_device(): rank_act = lax.psum(rank_part, 'tp').astype(jnp.bfloat16)  32.9 us
    dot_general x2, local copies, waits for them, and re-layouts, on_device(): jnp.dot(one_hot, pieces[0].reshape(piece_rows, -1), preferred_element_typ...  15.6 us
    all_to_all x1, starting transfers between devices, on_device(): lax.all_to_all(jnp.stack([bank_a] * lax.axis_size('blk')), 'blk', 0, 0)  11.1 us
    another operation x1, local copies, waits for them, and re-layouts, on_device(): pieces[0].reshape(piece_rows, -1)  10.5 us
  transfers between devices with their start and end apart: 5, of which 3 were waited for; matrix products, arithmetic and copies ran while one was open for 12% of the time, Pallas kernels for 0%

profile of v1, /device:TPU:1, one launch (start us, length us, event | category | flops | bytes accessed | tf_op | source)
XLA Modules:
  0.0 469.4 jit_solution(12672360994793539924)
XLA Ops:
  7.2 0.7 all-gather.5.cloned.1.call-update
  8.0 0.7 all-gather.3.cloned.1.call-update
  8.7 2.4 stack.2
  11.1 11.1 %all-to-all-start = ((bf16[32,1,1024,32]{2,3,1,0:T(8,128)(2,1)}), bf16[32,1,1024,32]{2,3,1,0:T(8,128)(2,1)S(1)}, u32[]{:S(2)}, u32[]{:S(2)}) async-start(bf16[32,1,1024,32]{2,3,1,0:T(8,128)(2,1)} %stack.2), calls=%async_computation.1 | async-start | bytes 4194304 | tf_op jit(solution)/shard_map/all_to_all | solution.py:28
  22.2 4.8 %fusion.45 = f32[256,2048]{1,0:T(8,128)} fusion(bf16[256,1024]{1,0:T(8,128)(2,1)S(1)} %copy-done, bf16[1024,2048]{1,0:T(8,128)(2,1)} %param.7), kind=kOutput, calls=%fused_computation.58 | convolution fusion | flops 1073741824 | bytes 6815744 | tf_op jit(solution)/shard_map/dot_general | solution.py:51
  27.1 44.2 %all-gather.5.cloned.1.call-done = bf16[256,2048]{1,0:T(8,128)(2,1)} async-done(((bf16[32,2048]{1,0:T(8,128)(2,1)}), bf16[256,2048]{1,0:T(8,128)(2,1)}) %all-gather.5.cloned.1.call-update) | async-done | bytes 1048592 | tf_op jit(solution)/shard_map/all_gather | solution.py:78
  71.3 2.1 fusion.43
  73.4 6.0 %copy.29 = bf16[32,1,1024,32]{3,2,0,1:T(8,128)(2,1)} copy(bf16[32,1,1024,32]{2,3,1,0:T(8,128)(2,1)S(1)} %all-to-all-done) | data formatting | bytes 4194304 | tf_op jit(solution)/shard_map/all_to_all | solution.py:28
  79.3 10.5 %reshape_reshape.3 = bf16[32,32768]{1,0:T(8,128)(2,1)S(1)} reshape(bf16[32,1,1024,32]{3,2,0,1:T(8,128)(2,1)} %copy.29) | data formatting | bytes 4194304 | tf_op jit(solution)/shard_map/reshape;reshape | solution.py:38
  89.9 8.0 %dot_general.58 = bf16[1024,32,32]{1,0,2:T(8,128)(2,1)} reshape(bf16[32768,32]{0,1:T(8,128)(2,1)S(1)} %bitcast.55) | data formatting | bytes 4194304 | tf_op jit(solution)/shard_map/dot_general | solution.py:37
  97.9 7.5 %copy.30 = bf16[1024,32,32]{0,2,1:T(8,128)(2,1)S(1)} copy(bf16[1024,32,32]{1,0,2:T(8,128)(2,1)} %dot_general.58) | data formatting | bytes 4194304 | tf_op jit(solution)/shard_map/dot_general | solution.py:37
  106.2 32.9 %psum.7 = bf16[2,128,32]{1,2,0:T(8,128)(2,1)S(1)} all-reduce(f32[2,128,32]{1,2,0:T(8,128)S(1)} %convolution_bitcast_fusion), channel_id=1, replica_groups=mesh['blk'=32,'tp'=8] {'tp'}, use_global_device_ids=true, to_apply=%region_1.0 | all-reduce | flops 8192 | bytes 49152 | tf_op jit(solution)/shard_map/psum | solution.py:49
  139.1 1.0 fusion.16
  140.3 3.9 fusion.5
  145.9 3.9 fusion.10
  149.9 0.6 copy-done.5
  152.3 1.7 copy-done.4
  154.4 2.1 fusion.3
  156.4 61.5 %reduce-scatter.2.cloned.1.call-done = f32[32,2048]{1,0:T(8,128)} async-done(((f32[256,2048]{1,0:T(8,128)}), f32[32,2048]{1,0:T(8,128)}) %reduce-scatter.2.cloned.1.call-update) | async-done | bytes 262160 | tf_op jit(solution)/shard_map/reduce_scatter | solution.py:50
  217.9 1.6 add_convert_fusion
  219.6 237.8 %all-reduce.3.cloned.1.call-done = f32[32,36864]{1,0:T(8,128)} async-done(((f32[32,36864]{1,0:T(8,128)}), f32[32,36864]{1,0:T(8,128)}) %all-reduce.3.cloned.1.call-update) | async-done | bytes 4718608
  457.4 2.2 dynamic-slice_reduce_fusion
  459.8 0.8 copy.39
  460.6 2.2 dynamic-slice.3
  (35 shorter events, 5.2 us)
Async XLA Ops:
  7.2 15.0 %copy-start = (bf16[256,1024]{1,0:T(8,128)(2,1)S(1)}, bf16[256,1024]{1,0:T(8,128)(2,1)}, u32[]{:S(2)}) copy-start(bf16[256,1024]{1,0:T(8,128)(2,1)} %param.6) | copy-start | bytes 1572868
  7.2 64.1 %all-gather.5.cloned.1.call-start = ((), (), s32[]{:S(2)}) async-start(), calls=%async_computation.4 | async-start | bytes 1179648 | tf_op jit(solution)/shard_map/all_gather | solution.py:78
  7.9 132.3 %all-gather.3.cloned.1.call-start = ((), (), s32[]{:S(2)}) async-start(), calls=%async_computation.3 | async-start | bytes 2162688 | tf_op jit(solution)/shard_map/all_gather | solution.py:30
  11.1 62.3 %all-to-all-start = ((bf16[32,1,1024,32]{2,3,1,0:T(8,128)(2,1)}), bf16[32,1,1024,32]{2,3,1,0:T(8,128)(2,1)S(1)}, u32[]{:S(2)}, u32[]{:S(2)}) async-start(bf16[32,1,1024,32]{2,3,1,0:T(8,128)(2,1)} %stack.2), calls=%async_computation.1 | async-start | bytes 4194304 | tf_op jit(solution)/shard_map/all_to_all | solution.py:28
  22.2 195.8 %reduce-scatter.2.cloned.1.call-start = ((), (), s32[]{:S(2)}) async-start(), calls=%async_computation.2 | async-start | bytes 2359296 | tf_op jit(solution)/shard_map/reduce_scatter | solution.py:50
  27.0 430.4 %all-reduce.3.cloned.1.call-start = ((), (), s32[]{:S(2)}) async-start(), calls=%async_computation.5 | async-start | bytes 9437184
  97.9 7.5 %copy-start.3 = (s32[2,1]{0,1:T(1,128)S(1)}, s32[2,1]{0,1:T(1,128)}, u32[]{:S(2)}) copy-start(s32[2,1]{0,1:T(1,128)} %param.10) | copy-start | bytes 28
  105.9 38.4 %copy-start.1 = (bf16[256,2048]{1,0:T(8,128)(2,1)S(1)}, bf16[256,2048]{1,0:T(8,128)(2,1)}, u32[]{:S(2)}) copy-start(bf16[256,2048]{1,0:T(8,128)(2,1)} %all-gather.5.cloned.1.call-done) | copy-start | bytes 3145732
  149.8 0.7 copy-start.5
  151.8 2.2 copy-start.4
  152.1 2.2 copy-start.2
Sparse Core Ops, SparseCore 0:
  10.7 60.5 all-gather.4
  73.1 62.7 all-gather.2
  139.9 77.9 reduce-scatter.1
  220.4 236.8 all-reduce.2
